TPU v7x, 128 devices: a whole 4x4x4 slice. The times are simulated.
128 devices in a mesh: dp: 8 (over z_hi, y), fsdp: 16 (over z_lo, x, core).
Axes of the slice: x: 4, y: 4, z: 4 (z_hi: 2, z_lo: 2; z = z_hi * 2 + z_lo), core: 2. Of those that a mesh axis runs over, the one named last changes fastest.
Arguments:
- weight: float32 [4096, 15360], P('fsdp', 'dp'), may hold values from -0.09375 to 0.09375
- history: float32 [7, 4096, 15360], P(None, 'fsdp', 'dp'), may hold values from -6 to 6
- newest: int32 [1], replicated, may hold values from 0 to 6
- band: float32 [8], replicated, may hold values from 0.5 to 1.5
- fresh: bfloat16 [4096, 15360], P('fsdp', 'dp'), may hold values from -6 to 6
- x_grad: bfloat16 [1024, 4096], P('dp', 'fsdp'), may hold values from -96 to 96
- dy_grad: bfloat16 [1024, 15360], P('dp'), may hold values from -6 to 6
- x_next: bfloat16 [6144, 4096], P('fsdp'), may hold values from -6 to 6
Outputs:
- new_weight: float32 [4096, 15360], P('fsdp', 'dp')
- noise_now: float32 [4096, 15360], P('fsdp', 'dp')
- next_out: bfloat16 [6144, 15360], P('fsdp', 'dp')
All inputs are finite; a program needn't handle non-finite values.
Results may differ from a plain program's by a relative error of at most 0.005.
Values may be sent and summed in bfloat16 or wider, within the bound.
A program may use at most 128 MiB of HBM per device.

v0:
```python
import math

import jax
import jax.numpy as jnp
from jax import lax
from jax.sharding import PartitionSpec as P

eps_value = 1e-06
learn_rate = 0.2
noise_multiplier = 0.01


def slot_weights(newest, band, slots):
    slot_index = jnp.arange(slots, dtype=jnp.int32)
    ages = (newest[0] - slot_index) % slots + 1
    table_index = jnp.arange(slots + 1, dtype=jnp.int32)
    return jnp.sum(jnp.where(ages[:, None] == table_index[None, :], band[None, :], 0.0), axis=1)


def local(weight, history, newest, band, fresh, x_grad, dy_grad, x_next):
    full_width = x_next.shape[1]
    hidden_units = dy_grad.shape[1]
    clip_bound = 2.0 * math.sqrt(full_width * hidden_units)
    x_float = x_grad.astype(jnp.float32)
    feature_sq = lax.psum(jnp.sum(x_float * x_float, axis=1), "fsdp")
    output_sq = jnp.sum(jnp.square(dy_grad.astype(jnp.float32)), axis=1)
    factor = jnp.minimum(1.0, clip_bound / jnp.sqrt(feature_sq * output_sq + eps_value))
    clipped = (factor[:, None] * x_float).astype(jnp.bfloat16)
    contract = (((0,), (0,)), ((), ()))
    partial_term = lax.dot_general(clipped, dy_grad, contract, preferred_element_type=jnp.float32)
    gradient = lax.psum_scatter(partial_term, "dp", scatter_dimension=1, tiled=True)
    tokens_all = x_grad.shape[0] * lax.axis_size("dp")
    slots = history.shape[0]
    mixing = slot_weights(newest, band, slots)
    combined = jnp.tensordot(mixing, history, axes=1, precision=lax.Precision.HIGHEST)
    noise_now = (fresh.astype(jnp.float32) - combined) / band[0]
    new_weight = (
        weight - learn_rate * (gradient + noise_multiplier * clip_bound * noise_now) / tokens_all
    )
    weight_half = new_weight.astype(jnp.bfloat16)
    next_float = jnp.dot(
        x_next,
        lax.all_gather(weight_half, "fsdp", axis=0, tiled=True),
        preferred_element_type=jnp.float32,
    )
    return (new_weight, noise_now, next_float.astype(jnp.bfloat16))


def solution(mesh):
    in_specs = (
        P("fsdp", "dp"),
        P(None, "fsdp", "dp"),
        P(),
        P(),
        P("fsdp", "dp"),
        P("dp", "fsdp"),
        P("dp", None),
        P("fsdp", None),
    )
    out_specs = (P("fsdp", "dp"), P("fsdp", "dp"), P("fsdp", "dp"))
    return jax.shard_map(local, mesh=mesh, in_specs=in_specs, out_specs=out_specs, check_vma=False)
```

profile of v0, /device:TPU:0, one launch (start us, length us, event | category | flops | bytes accessed | tf_op | source)
XLA Modules:
  0.0 341.9 jit_solution(2831296831227477096)
XLA Ops:
  7.2 0.0 copy-start
  7.2 0.0 copy-start.2
  7.2 0.0 reduce-scatter.2.cloned.1.call-start
  7.2 1.1 fusion.4
  8.3 30.8 %psum.7 = f32[128]{0:T(128)S(1)} all-reduce(f32[128]{0:T(128)S(1)} %fusion.4), channel_id=1, replica_groups=mesh['dp'=8,'fsdp'=16] {'fsdp'}, use_global_device_ids=true, to_apply=%region_1.0 | all-reduce | flops 128 | bytes 1024 | tf_op jit(solution)/shard_map/psum | solution.py:25
  39.1 0.0 copy-start.1
  39.1 3.1 multiply_reduce_fusion
  42.2 0.0 copy-done.2
  42.3 0.2 copy-done.1
  42.4 7.8 %fusion.6 = f32[256,15360]{1,0:T(8,128)} fusion(bf16[128,15360]{1,0:T(8,128)(2,1)S(1)} %copy-done.1, bf16[128,256]{1,0:T(8,128)(2,1)S(1)} %copy-done.2, f32[128]{0:T(128)S(1)} %multiply_minimum_fusion), kind=kOutput, calls=%fused_computation.12 | convolution fusion | flops 1006731264 | bytes 19726848 | tf_op jit(solution)/shard_map/dot_general | solution.py:30
  50.2 0.0 copy-start.3
  50.2 0.0 reduce-scatter.2.cloned.1.call-update
  50.3 0.0 all-gather.2.cloned.1.call-start
  51.0 0.0 copy-done.3
  51.0 0.2 select_reduce_fusion
  51.2 27.8 %fusion = f32[1,256,1920]{2,0,1:T(1,128)} fusion(f32[7,256,1920]{2,1,0:T(8,128)} %param.9, f32[7]{0:T(128)S(1)} %select_reduce_fusion), kind=kOutput, calls=%fused_computation | convolution fusion | flops 41287680 | bytes 15728668 | tf_op jit(solution)/shard_map/dot_general | solution.py:35
  78.9 150.3 %reduce-scatter.2.cloned.1.call-done = f32[256,1920]{1,0:T(8,128)} async-done(((f32[256,15360]{1,0:T(8,128)}), f32[256,1920]{1,0:T(8,128)}) %reduce-scatter.2.cloned.1.call-update) | async-done | bytes 1966096 | tf_op jit(solution)/shard_map/reduce_scatter | solution.py:31
  229.2 5.7 %fusion.11 = (bf16[256,1920]{1,0:T(8,128)(2,1)}, f32[256,1920]{1,0:T(8,128)}, f32[256,1920]{1,0:T(8,128)}) fusion(f32[256,1920]{1,0:T(8,128)} %param.8, f32[256,1920]{1,0:T(8,128)} %reduce-scatter.2.cloned.1.call-done, f32[]{:T(128)S(1)} %bitcast.17, f32[1,256,1920]{2,0,1:T(1,128)} %fusion, bf16[256,1920]{1,0:T(8,128)(2,1)} %param.12), kind=kLoop, calls=%fused_computation.20 | loop fusion | flops 3932160 | bytes 11796484 | tf_op jit(solution)/shard_map/convert_element_type | solution.py:40
  234.9 0.0 all-gather.2.cloned.1.call-update
  235.0 84.5 %all-gather.2.cloned.1.call-done = bf16[4096,1920]{1,0:T(8,128)(2,1)} async-done(((bf16[256,1920]{1,0:T(8,128)(2,1)}), bf16[4096,1920]{1,0:T(8,128)(2,1)}) %all-gather.2.cloned.1.call-update) | async-done | bytes 15728656 | tf_op jit(solution)/shard_map/all_gather | solution.py:43
  319.4 0.0 copy-done
  319.4 13.1 %fusion.2 = bf16[384,1920]{0,1:T(8,128)(2,1)} fusion(bf16[4096,1920]{1,0:T(8,128)(2,1)} %all-gather.2.cloned.1.call-done, bf16[384,4096]{1,0:T(8,128)(2,1)S(1)} %copy-done), kind=kOutput, calls=%fused_computation.4 | convolution fusion | flops 6040535040 | bytes 20348928 | tf_op jit(solution)/shard_map/dot_general | solution.py:41
  332.6 2.5 copy.12
  (2 shorter events, 0.0 us)
Async XLA Ops:
  7.2 312.3 %copy-start = (bf16[384,4096]{1,0:T(8,128)(2,1)S(1)}, bf16[384,4096]{1,0:T(8,128)(2,1)}, u32[]{:S(2)}) copy-start(bf16[384,4096]{1,0:T(8,128)(2,1)} %param.15) | copy-start | bytes 9437188
  7.2 35.1 %copy-start.2 = (bf16[128,256]{1,0:T(8,128)(2,1)S(1)}, bf16[128,256]{1,0:T(8,128)(2,1)}, u32[]{:S(2)}) copy-start(bf16[128,256]{1,0:T(8,128)(2,1)} %param.13) | copy-start | bytes 196612
  7.2 222.0 %reduce-scatter.2.cloned.1.call-start = ((), (), s32[]{:S(2)}) async-start(), calls=%async_computation.1 | async-start | bytes 17694720 | tf_op jit(solution)/shard_map/reduce_scatter | solution.py:31
  39.1 3.3 copy-start.1
  50.2 0.7 copy-start.3
  50.3 269.2 %all-gather.2.cloned.1.call-start = ((), (), s32[]{:S(2)}) async-start(), calls=%async_computation.2 | async-start | bytes 16711680 | tf_op jit(solution)/shard_map/all_gather | solution.py:43
Sparse Core Ops, SparseCore 0:
  50.4 178.7 reduce-scatter.1
  235.1 84.3 all-gather.1
where the time goes:
time: 343 us; the launch traced here: 342 us
  waiting for transfers between devices  235 us (69%)
  matrix products  48.7 us (14%)
  blocking collectives  30.8 us (9%)
  between operations  14.7 us (4%)
  other arithmetic  10.1 us (3%)
    reduce_scatter x1, waiting for transfers between devices, local(): lax.psum_scatter(partial_term, 'dp', scatter_dimension=1, tiled=True)  150 us
    all_gather x1, waiting for transfers between devices, local(): lax.all_gather(weight_half, 'fsdp', axis=0, tiled=True)  84.5 us
    psum x1, blocking collectives, local(): feature_sq = lax.psum(jnp.sum(x_float * x_float, axis=1), 'fsdp')  30.8 us
    dot_general x1, matrix products, local(): jnp.tensordot(mixing, history, axes=1, precision=lax.Precision.HIGHEST)  27.8 us
    dot_general x1, matrix products, local(): jnp.dot(x_next, lax.all_gather(weight_half, 'fsdp', axis=0, tiled=True),...  13.1 us
    dot_general x1, matrix products, local(): lax.dot_general(clipped, dy_grad, contract, preferred_element_type=jnp.fl...  7.81 us
  transfers between devices with their start and end apart: 2, of which 2 were waited for; matrix products, arithmetic and copies ran while one was open for 8% of the time, Pallas kernels for 0%

commit v1 on v0

--- a/solution.py
+++ b/solution.py
@@ -21,14 +21,15 @@
     full_width = x_next.shape[1]
     hidden_units = dy_grad.shape[1]
     clip_bound = 2.0 * math.sqrt(full_width * hidden_units)
+    dy_mine = lax.all_to_all(dy_grad, "dp", split_axis=1, concat_axis=0, tiled=True)
     x_float = x_grad.astype(jnp.float32)
     feature_sq = lax.psum(jnp.sum(x_float * x_float, axis=1), "fsdp")
     output_sq = jnp.sum(jnp.square(dy_grad.astype(jnp.float32)), axis=1)
     factor = jnp.minimum(1.0, clip_bound / jnp.sqrt(feature_sq * output_sq + eps_value))
     clipped = (factor[:, None] * x_float).astype(jnp.bfloat16)
+    clipped_all = lax.all_gather(clipped, "dp", axis=0, tiled=True)
     contract = (((0,), (0,)), ((), ()))
-    partial_term = lax.dot_general(clipped, dy_grad, contract, preferred_element_type=jnp.float32)
-    gradient = lax.psum_scatter(partial_term, "dp", scatter_dimension=1, tiled=True)
+    gradient = lax.dot_general(clipped_all, dy_mine, contract, preferred_element_type=jnp.float32)
     tokens_all = x_grad.shape[0] * lax.axis_size("dp")
     slots = history.shape[0]
     mixing = slot_weights(newest, band, slots)

time: 343 us -> 261 us (0.76)
  waiting for transfers between devices: 235 us -> 86.3 us
  blocking collectives: 30.8 us -> 83.7 us
  local copies, waits for them, and re-layouts: 2.73 us -> 15.4 us
  starting transfers between devices: 0.08 us -> 8.06 us
  other arithmetic: 10.1 us -> 4.86 us
    reduce_scatter x1 -> x0, waiting for transfers between devices: 150 us -> none  [local(): lax.psum_scatter(partial_term, 'dp', scatter_dimension=1, tiled=True)]
    all_gather x0 -> x1, blocking collectives: none -> 47.8 us  [local(): clipped_all = lax.all_gather(clipped, 'dp', axis=0, tiled=True)]
    all_to_all x0 -> x1, starting transfers between devices: none -> 8.03 us  [local(): lax.all_to_all(dy_grad, 'dp', split_axis=1, concat_axis=0, tiled=True)]
    all_to_all x0 -> x1, local copies, waits for them, and re-layouts: none -> 6.38 us  [local(): lax.all_to_all(dy_grad, 'dp', split_axis=1, concat_axis=0, tiled=True)]
    unnamed x9 -> x10, local copies, waits for them, and re-layouts: 2.73 us -> 8.98 us
    convert_element_type x1, other arithmetic: 5.74 us -> 0.1 us  [local(): clipped = (factor[:, None] * x_float).astype(jnp.bfloat16)]
    psum x1, blocking collectives: 30.8 us -> 35.9 us  [local(): feature_sq = lax.psum(jnp.sum(x_float * x_float, axis=1), 'fsdp')]
  transfers between devices with their start and end apart: 2 -> 2, of which waited for: 2 -> 1; matrix products, arithmetic and copies ran while one was open for 8% -> 12% of each run, Pallas kernels for 0% -> 0%
where the time goes in v1:
time: 261 us; the launch traced here: 259 us
  waiting for transfers between devices  86.3 us (33%)
  blocking collectives  83.7 us (32%)
  matrix products  46.4 us (18%)
  local copies, waits for them, and re-layouts  15.4 us (6%)
  between operations  14.7 us (6%)
  starting transfers between devices  8.06 us (3%)
  other arithmetic  4.86 us (2%)
    all_gather x1, waiting for transfers between devices, local(): lax.all_gather(weight_half, 'fsdp', axis=0, tiled=True)  86.3 us
    all_gather x1, blocking collectives, local(): clipped_all = lax.all_gather(clipped, 'dp', axis=0, tiled=True)  47.8 us
    psum x1, blocking collectives, local(): feature_sq = lax.psum(jnp.sum(x_float * x_float, axis=1), 'fsdp')  35.9 us
    dot_general x1, matrix products, local(): jnp.tensordot(mixing, history, axes=1, precision=lax.Precision.HIGHEST)  26.8 us
    dot_general x1, matrix products, local(): jnp.dot(x_next, lax.all_gather(weight_half, 'fsdp', axis=0, tiled=True),...  13.1 us
    unnamed x10, local copies, waits for them, and re-layouts  8.98 us
    all_to_all x1, starting transfers between devices, local(): lax.all_to_all(dy_grad, 'dp', split_axis=1, concat_axis=0, tiled=True)  8.03 us
    dot_general x1, matrix products, local(): lax.dot_general(clipped_all, dy_mine, contract, preferred_element_type=jn...  6.44 us
  transfers between devices with their start and end apart: 2, of which 1 were waited for; matrix products, arithmetic and copies ran while one was open for 12% of the time, Pallas kernels for 0%

profile of v1, /device:TPU:0, one launch (start us, length us, event | category | flops | bytes accessed | tf_op | source)
XLA Modules:
  0.0 259.4 jit_solution(6377903200026531716)
XLA Ops:
  7.2 0.0 copy-start
  7.2 6.4 %copy.16 = bf16[128,15360]{0,1:T(8,128)(2,1)} copy(bf16[128,15360]{1,0:T(8,128)(2,1)} %param.14) | data formatting | bytes 7864320 | tf_op args[6]
  13.6 0.0 copy-start.2
  13.6 0.0 copy-start.3
  13.6 8.0 %all-to-all-start = ((bf16[128,8,1920]{0,2,1:T(8,128)(2,1)}), bf16[128,8,1920]{0,2,1:T(8,128)(2,1)}, u32[]{:S(2)}, u32[]{:S(2)}) async-start(bf16[128,8,1920]{0,2,1:T(8,128)(2,1)} %bitcast.20), calls=%async_computation | async-start | bytes 7864320 | tf_op jit(solution)/shard_map/all_to_all | solution.py:24
  21.6 0.0 all-gather.2.cloned.1.call-start
  22.3 0.0 copy-done.2
  22.3 0.1 fusion.6
  22.4 35.9 %psum.7 = f32[128]{0:T(128)S(1)} all-reduce(f32[128]{0:T(128)S(1)} %fusion.6), channel_id=1, replica_groups=mesh['dp'=8,'fsdp'=16] {'fsdp'}, use_global_device_ids=true, to_apply=%region_1.0 | all-reduce | flops 128 | bytes 1024 | tf_op jit(solution)/shard_map/psum | solution.py:26
  58.3 0.0 copy-done.3
  58.3 0.2 select_reduce_fusion
  58.5 3.0 %multiply_reduce_fusion = f32[128]{0:T(128)S(1)} fusion(bf16[128,15360]{1,0:T(8,128)(2,1)} %param.14), kind=kLoop, calls=%fused_computation.2 | loop fusion | flops 5898112 | bytes 3932672 | tf_op jit(solution)/shard_map/reduce_sum | solution.py:27
  61.5 0.1 fusion.7
  61.6 47.8 %all_gather.6 = bf16[1024,256]{1,0:T(8,128)(2,1)} all-gather(bf16[128,256]{1,0:T(8,128)(2,1)S(1)} %fusion.7), channel_id=1, replica_groups=mesh['dp'=8,'fsdp'=16] {'dp'}, dimensions={0}, use_global_device_ids=true | all-gather | bytes 589824 | tf_op jit(solution)/shard_map/all_gather | solution.py:30
  109.4 0.0 copy-start.1
  109.4 26.8 %fusion = f32[1,256,1920]{2,0,1:T(1,128)S(1)} fusion(f32[7,256,1920]{2,1,0:T(8,128)} %param.9, f32[7]{0:T(128)S(1)} %select_reduce_fusion), kind=kOutput, calls=%fused_computation | convolution fusion | flops 41287680 | bytes 15728668 | tf_op jit(solution)/shard_map/dot_general | solution.py:36
  136.2 0.0 copy-done.1
  136.2 1.5 fusion.5
  137.7 0.0 all-to-all-done
  137.7 6.4 %copy.17 = bf16[8,128,1920]{2,1,0:T(8,128)(2,1)} copy(bf16[8,128,1920]{1,2,0:T(8,128)(2,1)} %bitcast.1) | data formatting | bytes 7864320 | tf_op jit(solution)/shard_map/all_to_all | solution.py:24
  144.1 6.4 %fusion.10 = (bf16[256,1920]{1,0:T(8,128)(2,1)}, f32[256,1920]{1,0:T(8,128)}) fusion(f32[256,1920]{1,0:T(8,128)} %param.8, f32[256,1920]{1,0:T(8,128)} %fusion.5, bf16[1024,256]{1,0:T(8,128)(2,1)} %all_gather.6, bf16[1024,1920]{1,0:T(8,128)(2,1)} %bitcast.21), kind=kOutput, calls=%fused_computation.20 | convolution fusion | flops 1009090560 | bytes 11337728 | tf_op jit(solution)/shard_map/dot_general | solution.py:32
  150.5 0.0 all-gather.2.cloned.1.call-update
  150.6 86.3 %all-gather.2.cloned.1.call-done = bf16[4096,1920]{1,0:T(8,128)(2,1)} async-done(((bf16[256,1920]{1,0:T(8,128)(2,1)}), bf16[4096,1920]{1,0:T(8,128)(2,1)}) %all-gather.2.cloned.1.call-update) | async-done | bytes 15728656 | tf_op jit(solution)/shard_map/all_gather | solution.py:44
  236.9 0.0 copy-done
  236.9 13.1 %fusion.4 = bf16[384,1920]{0,1:T(8,128)(2,1)} fusion(bf16[4096,1920]{1,0:T(8,128)(2,1)} %all-gather.2.cloned.1.call-done, bf16[384,4096]{1,0:T(8,128)(2,1)S(1)} %copy-done), kind=kOutput, calls=%fused_computation.7 | convolution fusion | flops 6040535040 | bytes 20348928 | tf_op jit(solution)/shard_map/dot_general | solution.py:42
  250.0 2.5 copy.18
  (2 shorter events, 0.0 us)
Async XLA Ops:
  7.2 229.7 %copy-start = (bf16[384,4096]{1,0:T(8,128)(2,1)S(1)}, bf16[384,4096]{1,0:T(8,128)(2,1)}, u32[]{:S(2)}) copy-start(bf16[384,4096]{1,0:T(8,128)(2,1)} %param.15) | copy-start | bytes 9437188
  13.6 8.7 %copy-start.2 = (bf16[128,256]{1,0:T(8,128)(2,1)S(1)}, bf16[128,256]{1,0:T(8,128)(2,1)}, u32[]{:S(2)}) copy-start(bf16[128,256]{1,0:T(8,128)(2,1)} %param.13) | copy-start | bytes 196612
  13.6 44.7 %copy-start.3 = (f32[8]{0:T(128)S(1)}, f32[8]{0:T(128)}, u32[]{:S(2)}) copy-start(f32[8]{0:T(128)} %param.11) | copy-start | bytes 100
  13.6 124.1 %all-to-all-start = ((bf16[128,8,1920]{0,2,1:T(8,128)(2,1)}), bf16[128,8,1920]{0,2,1:T(8,128)(2,1)}, u32[]{:S(2)}, u32[]{:S(2)}) async-start(bf16[128,8,1920]{0,2,1:T(8,128)(2,1)} %bitcast.20), calls=%async_computation | async-start | bytes 7864320 | tf_op jit(solution)/shard_map/all_to_all | solution.py:24
  21.6 215.2 %all-gather.2.cloned.1.call-start = ((), (), s32[]{:S(2)}) async-start(), calls=%async_computation.1 | async-start | bytes 16711680 | tf_op jit(solution)/shard_map/all_gather | solution.py:44
  109.4 26.9 %copy-start.1 = (bf16[256,1920]{1,0:T(8,128)(2,1)S(1)}, bf16[256,1920]{1,0:T(8,128)(2,1)}, u32[]{:S(2)}) copy-start(bf16[256,1920]{1,0:T(8,128)(2,1)} %param.12) | copy-start | bytes 2949124
Sparse Core Ops, SparseCore 0:
  150.7 86.1 all-gather.1

commit v2 on v0

v2 whole, which is shorter than its diff:
```python
import functools
import math

import jax
import jax.numpy as jnp
from jax import lax
from jax.experimental import pallas as pl
from jax.experimental.pallas import tpu as pltpu
from jax.sharding import PartitionSpec as P

eps_value = 1e-06
learn_rate = 0.2
noise_multiplier = 0.01

LANES = 128
ROWS_IN = 224
PIECES = 4
LAG_B, LAG_C, LAG_D, LAG_E, LAG_F = 1, 3, 4, 6, 8
EARLY = 5
MESH = pl.DeviceIdType.MESH


def wait_for(ref, sem):
    pltpu.make_async_copy(ref, ref, sem).wait()


def kernel(
    clip_bound, tokens_all,
    newest, band, weight, history, fresh, x_grad, dy_grad, x_next,
    new_weight, noise_now, next_out,
    hist, wv, fr, dyb, wb, xo, xp, psend, precv, own, obuf, xg, dyq, cts, sbuf, rbuf,
    s_hist, s_wv, s_fr, s_dyr, s_dyf, s_left, s_right, s_opp, s_sib, s_part, s_stat_s, s_stat_r, s_misc,
):
    chunks = hist.shape[0]
    slots = hist.shape[1]
    half = xo.shape[1]
    units = chunks * LANES
    d, f = lax.axis_index("dp"), lax.axis_index("fsdp")
    hi, y = d // 4, d % 4
    lo, x, c = f // 8, (f // 2) % 4, f % 2
    oc = 1 - c
    xr, xl, xx = (x + 1) % 4, (x + 3) % 4, (x + 2) % 4

    def at(lo_, x_, c_):
        return (d, lo_ * 8 + x_ * 2 + c_)

    sibling = at(lo, x, oc)
    right, left = at(lo, xr, c), at(lo, xl, c)
    inner = at(1 - lo, x, c)
    flipped = (1 - lo) * 8 + x * 2 + c
    outer = ((1 - hi) * 4 + y, flipped)
    same_hi = [(hi * 4 + (y + s) % 4, f) for s in (1, 3, 2)]
    other_hi = [((1 - hi) * 4 + (y + s) % 4, flipped) for s in (0, 1, 3, 2)]
    other_hi_same_f = [((1 - hi) * 4 + (y + s) % 4, f) for s in (0, 1, 3, 2)]

    (S_XG, S_DYQ, S_XO, S_XIN, S_XOUT, S_CT, S_DYS, S_DYFS, S_W1, S_W2, S_W3, S_PS, S_XS1, S_XS2, S_CTS,
     S_ONW, S_ONN, S_OUT) = range(18)

    def cols(k):
        return pl.ds(pl.multiple_of(k * LANES, LANES), LANES)

    def remote(src, dst, send, recv, to):
        pltpu.make_async_remote_copy(src, dst, send, recv, device_id=to, device_id_type=MESH).start()

    barrier = pltpu.get_barrier_semaphore()
    peers = [sibling, right, left, inner] + same_hi + other_hi_same_f + other_hi
    for peer in peers:
        pl.semaphore_signal(barrier, inc=1, device_id=peer, device_id_type=MESH)

    share = f // 2
    pltpu.make_async_copy(x_grad, xg, s_misc.at[S_XG]).start()
    pltpu.make_async_copy(
        dy_grad.at[:, pl.ds(pl.multiple_of(share * units, LANES), units)], dyq, s_misc.at[S_DYQ]
    ).start()

    def fetch(k):
        pltpu.make_async_copy(history.at[:, :, cols(k)], hist.at[k], s_hist.at[k]).start()
        pltpu.make_async_copy(weight.at[:, cols(k)], wv.at[k], s_wv.at[k]).start()
        pltpu.make_async_copy(fresh.at[:, cols(k)], fr.at[k], s_fr.at[k]).start()

    my_rows = pl.ds(pl.multiple_of(c * 64, 64), 64)

    def fetch_dy(k):
        column = pl.ds(pl.multiple_of(d * units + k * LANES, LANES), LANES)
        pltpu.make_async_copy(dy_grad.at[my_rows, column], dyb.at[k, d, c], s_dyr.at[k]).start()

    @pl.loop(0, 2)
    def _(k):
        fetch_dy(k)
        fetch(k)

    wait_for(xg, s_misc.at[S_XG])
    x_t = xg[...].astype(jnp.float32).T
    feature_part = jnp.sum(x_t * x_t, axis=0, keepdims=True)
    wait_for(dyq, s_misc.at[S_DYQ])
    total = jnp.zeros((LANES, LANES), jnp.float32)
    for n in range(chunks):
        piece = dyq[:, n * LANES : (n + 1) * LANES].astype(jnp.float32)
        total = total + piece * piece
    output_part = 0.5 * jnp.sum(total.T, axis=0, keepdims=True)
    row = lax.broadcasted_iota(jnp.int32, (8, LANES), 0)
    sbuf[0] = jnp.where(row == 0, feature_part, jnp.where(row == 1, output_part, 0.0))

    pl.semaphore_wait(barrier, len(peers))

    def stat_send(r, to):
        remote(sbuf.at[r], rbuf.at[r], s_stat_s.at[r], s_stat_r.at[r], to)

    def stat_take(r):
        wait_for(rbuf.at[r], s_stat_r.at[r])
        sbuf[r + 1] = sbuf[r] + rbuf[r]

    def send_dy_to(k, to):
        column = pl.ds(pl.multiple_of(to[0] * units + k * LANES, LANES), LANES)
        remote(dy_grad.at[my_rows, column], dyb.at[k, d, c], s_misc.at[S_DYS], s_dyr.at[k], to)

    def send_dy(k):
        for to in other_hi + same_hi:
            send_dy_to(k, to)

    stat_send(0, sibling)
    send_dy(0)
    stat_take(0)
    stat_send(1, at(lo, x + 1 - 2 * (x % 2), c))
    other_half = pl.multiple_of((1 - lo) * half, LANES)
    remote(
        x_next.at[0:ROWS_IN, pl.ds(other_half, half)], xp.at[0:ROWS_IN], s_misc.at[S_XS1], s_misc.at[S_XIN], inner
    )
    send_dy(1)
    stat_take(1)
    stat_send(2, at(lo, 3 - x, c))
    width = half // PIECES

    def send_piece(q):
        remote(
            x_next.at[ROWS_IN:, pl.ds(pl.multiple_of(other_half + q * width, LANES), width)],
            xp.at[ROWS_IN:, pl.ds(pl.multiple_of(q * width, LANES), width)],
            s_misc.at[S_XS2], s_misc.at[S_XOUT], outer,
        )

    stat_take(2)
    stat_send(3, inner)

    @pl.loop(2, EARLY)
    def _(k):
        send_dy(k)
        send_piece(k - 2)

    stat_take(3)
    both = sbuf[4]
    factor = jnp.minimum(1.0, clip_bound / jnp.sqrt(both[0:1] * both[1:2] + eps_value))
    mine = pl.ds(pl.multiple_of(d * LANES, LANES), LANES)
    cts[:, mine] = (x_t * factor).astype(jnp.bfloat16)
    for to in other_hi_same_f + same_hi:
        remote(cts.at[:, mine], cts.at[:, mine], s_misc.at[S_CTS], s_misc.at[S_CT], to)

    for q in range(EARLY - 2, PIECES):
        send_piece(q)

    @pl.loop(EARLY, chunks)
    def _(k):
        send_dy(k)

    pltpu.make_async_copy(x_next.at[:, pl.ds(pl.multiple_of(lo * half, LANES), half)], xo, s_misc.at[S_XO]).start()

    @pl.loop(2, chunks)
    def _(k):
        fetch_dy(k)
        fetch(k)

    first = newest[0]
    mixing = [band[lax.rem(first + (slots - s), slots) + 1] for s in range(slots)]
    now_coefficient = band[0]

    wait_for(cts.at[:, 0 : 7 * LANES], s_misc.at[S_CT])

    def stage_a(k):
        wait_for(dyb.at[k, :, c], s_dyr.at[k])
        remote(dyb.at[k, :, c], dyb.at[k, :, c], s_misc.at[S_DYFS], s_dyf.at[k], sibling)

    def stage_b(k):
        wait_for(hist.at[k], s_hist.at[k])
        wait_for(wv.at[k], s_wv.at[k])
        wait_for(fr.at[k], s_fr.at[k])
        combined = mixing[0] * hist[k, 0]
        for s in range(1, slots):
            combined = combined + mixing[s] * hist[k, s]
        noise = (fr[k].astype(jnp.float32) - combined) / jnp.full(combined.shape, now_coefficient, jnp.float32)
        hist[k, 0] = noise
        wait_for(dyb.at[k, :, oc], s_dyf.at[k])
        gradient = jnp.dot(cts[...], dyb[k].reshape(8 * LANES, LANES), preferred_element_type=jnp.float32)
        updated = wv[k] - learn_rate * (gradient + (noise_multiplier * clip_bound) * noise) * (1.0 / tokens_all)
        wb[k, x, c] = updated.astype(jnp.bfloat16)
        wv[k] = updated
        block = wb.at[k, x, c]
        remote(block, block, s_misc.at[S_W1], s_left.at[k], right)
        remote(block, block, s_misc.at[S_W1], s_right.at[k], left)
        remote(block, block, s_misc.at[S_W1], s_sib.at[k], sibling)
        pltpu.make_async_copy(hist.at[k, 0], noise_now.at[:, cols(k)], s_misc.at[S_ONN]).start()
        pltpu.make_async_copy(wv.at[k], new_weight.at[:, cols(k)], s_misc.at[S_ONW]).start()

    upper, lower = pl.ds(0, LANES), pl.ds(LANES, LANES)

    def stage_c(k):
        from_left, from_right = wb.at[k, xl, c], wb.at[k, xr, c]
        wait_for(from_left, s_left.at[k])
        top = wb.at[k, xl, c, upper]
        remote(top, top, s_misc.at[S_W2], s_opp.at[k], right)
        remote(from_left, from_left, s_misc.at[S_W3], s_sib.at[k], sibling)
        wait_for(from_right, s_right.at[k])
        bottom = wb.at[k, xr, c, lower]
        remote(bottom, bottom, s_misc.at[S_W2], s_opp.at[k], left)
        remote(from_right, from_right, s_misc.at[S_W3], s_sib.at[k], sibling)

    def stage_d(k):
        block = wb.at[k, xx, c]
        wait_for(block, s_opp.at[k])
        remote(block, block, s_misc.at[S_W3], s_sib.at[k], sibling)

    def multiply(ks):
        parts = [wb[k].reshape(half, LANES) for k in ks]
        rhs = parts[0] if len(ks) == 1 else jnp.concatenate(parts, axis=1)
        theirs = jnp.dot(xp[...], rhs, preferred_element_type=jnp.float32).astype(jnp.bfloat16)
        for n, k in enumerate(ks):
            psend[k] = theirs[:, n * LANES : (n + 1) * LANES]
            remote(psend.at[k], precv.at[k], s_misc.at[S_PS], s_part.at[k], inner)
        ours = jnp.dot(xo[...], rhs, preferred_element_type=jnp.float32)
        for n, k in enumerate(ks):
            own[k] = ours[:, n * LANES : (n + 1) * LANES]

    def stage_e(k):
        @pl.when(k == 0)
        def _():
            wait_for(xo, s_misc.at[S_XO])
            wait_for(xp.at[0:ROWS_IN], s_misc.at[S_XIN])
            wait_for(xp.at[ROWS_IN:], s_misc.at[S_XOUT])

        wait_for(wb.at[k, :, oc], s_sib.at[k])

        @pl.when(k % 2 == 1)
        def _():
            multiply((k - 1, k))

        if chunks % 2 == 1:

            @pl.when(k == chunks - 1)
            def _():
                multiply((k,))

    def stage_f(k):
        wait_for(precv.at[k], s_part.at[k])
        obuf[k] = (own[k] + precv[k].astype(jnp.float32)).astype(jnp.bfloat16)
        pltpu.make_async_copy(obuf.at[k], next_out.at[:, cols(k)], s_misc.at[S_OUT]).start()

    def staged(stage, t, lag):
        k = t - lag

        @pl.when((k >= 0) & (k < chunks))
        def _():
            stage(k)

    @pl.loop(0, chunks + LAG_F)
    def _(t):
        staged(stage_c, t, LAG_C)
        staged(stage_d, t, LAG_D)
        staged(stage_a, t, 0)
        staged(stage_b, t, LAG_B)
        staged(stage_e, t, LAG_E)
        staged(stage_f, t, LAG_F)

    for r in range(4):
        wait_for(sbuf.at[r], s_stat_s.at[r])
    wait_for(dyb.at[:, 0:7, 0], s_misc.at[S_DYS])
    wait_for(dyb.at[:, :, 0], s_misc.at[S_DYFS])
    wait_for(xp.at[0:ROWS_IN], s_misc.at[S_XS1])
    wait_for(xp.at[ROWS_IN:], s_misc.at[S_XS2])
    wait_for(cts.at[:, 0 : 7 * LANES], s_misc.at[S_CTS])
    wait_for(wb.at[:, 0:3, 0], s_misc.at[S_W1])
    wait_for(wb.at[:, 0, 0], s_misc.at[S_W2])
    wait_for(wb.at[:, 0:3, 0], s_misc.at[S_W3])
    wait_for(psend, s_misc.at[S_PS])
    wait_for(hist.at[:, 0], s_misc.at[S_ONN])
    wait_for(wv, s_misc.at[S_ONW])
    wait_for(obuf, s_misc.at[S_OUT])


def local(weight, history, newest, band, fresh, x_grad, dy_grad, x_next):
    slots, rows, units = history.shape
    tokens, full_width = x_next.shape
    hidden_units = dy_grad.shape[1]
    clip_bound = 2.0 * math.sqrt(full_width * hidden_units)
    tokens_all = x_grad.shape[0] * lax.axis_size("dp")
    chunks = units // LANES
    half = full_width // 2
    any_space = pl.BlockSpec(memory_space=pl.ANY)
    scalars = pl.BlockSpec(memory_space=pltpu.SMEM)
    f32, b16 = jnp.float32, jnp.bfloat16
    per_chunk = pltpu.SemaphoreType.DMA((chunks,))
    return pl.pallas_call(
        functools.partial(kernel, clip_bound, tokens_all),
        out_shape=(
            jax.ShapeDtypeStruct((rows, units), f32),
            jax.ShapeDtypeStruct((rows, units), f32),
            jax.ShapeDtypeStruct((tokens, units), b16),
        ),
        in_specs=[scalars, scalars] + [any_space] * 6,
        out_specs=(any_space,) * 3,
        scratch_shapes=[
            pltpu.VMEM((chunks, slots, rows, LANES), f32),
            pltpu.VMEM((chunks, rows, LANES), f32),
            pltpu.VMEM((chunks, rows, LANES), b16),
            pltpu.VMEM((chunks, 8, 2, 64, LANES), b16),
            pltpu.VMEM((chunks, 4, 2, rows, LANES), b16),
            pltpu.VMEM((tokens, half), b16),
            pltpu.VMEM((tokens, half), b16),
            pltpu.VMEM((chunks, tokens, LANES), b16),
            pltpu.VMEM((chunks, tokens, LANES), b16),
            pltpu.VMEM((chunks, tokens, LANES), f32),
            pltpu.VMEM((chunks, tokens, LANES), b16),
            pltpu.VMEM(x_grad.shape, b16),
            pltpu.VMEM((x_grad.shape[0], units), b16),
            pltpu.VMEM((rows, tokens_all), b16),
            pltpu.VMEM((5, 8, LANES), f32),
            pltpu.VMEM((4, 8, LANES), f32),
        ]
        + [per_chunk] * 10
        + [pltpu.SemaphoreType.DMA((4,)), pltpu.SemaphoreType.DMA((4,)), pltpu.SemaphoreType.DMA((18,))],
        compiler_params=pltpu.CompilerParams(
            collective_id=0, has_side_effects=True, vmem_limit_bytes=67043328
        ),
        name="step",
    )(newest, band, weight, history, fresh, x_grad, dy_grad, x_next)


def solution(mesh):
    in_specs = (
        P("fsdp", "dp"),
        P(None, "fsdp", "dp"),
        P(),
        P(),
        P("fsdp", "dp"),
        P("dp", "fsdp"),
        P("dp", None),
        P("fsdp", None),
    )
    out_specs = (P("fsdp", "dp"), P("fsdp", "dp"), P("fsdp", "dp"))
    return jax.shard_map(local, mesh=mesh, in_specs=in_specs, out_specs=out_specs, check_vma=False)
```

time: 343 us -> 109 us (0.32)
  waiting for transfers between devices: 235 us -> 0 us
  Pallas kernels: 0 us -> 102 us
  matrix products: 48.7 us -> 0 us
  blocking collectives: 30.8 us -> 0 us
  between operations: 14.7 us -> 1.3 us
  other arithmetic: 10.1 us -> 0 us
  local copies, waits for them, and re-layouts: 2.73 us -> 6.28 us
    reduce_scatter x1 -> x0, waiting for transfers between devices: 150 us -> none  [local(): lax.psum_scatter(partial_term, 'dp', scatter_dimension=1, tiled=True)]
    pallas_call x0 -> x1, Pallas kernels: none -> 102 us  [local(): pl.pallas_call(functools.partial(kernel, clip_bound, tokens_all), out_sha...]
    all_gather x1 -> x0, waiting for transfers between devices: 84.5 us -> none  [local(): lax.all_gather(weight_half, 'fsdp', axis=0, tiled=True)]
    dot_general x3 -> x0, matrix products: 48.7 us -> none  [the longest x1 27.8 us: local(): jnp.tensordot(mixing, history, axes=1, precision=lax.Precision.HIGHEST)]
    psum x1 -> x0, blocking collectives: 30.8 us -> none  [local(): feature_sq = lax.psum(jnp.sum(x_float * x_float, axis=1), 'fsdp')]
    convert_element_type x1 -> x0, other arithmetic: 5.74 us -> none  [local(): weight_half = new_weight.astype(jnp.bfloat16)]
    reduce_sum x3 -> x0, other arithmetic: 4.38 us -> none  [the longest x1 3.1 us: local(): output_sq = jnp.sum(jnp.square(dy_grad.astype(jnp.float32)), axis=1)]
    unnamed x9 -> x7, local copies, waits for them, and re-layouts: 2.73 us -> 6.28 us
  transfers between devices with their start and end apart: 2 -> 0, of which waited for: 2 -> 0; matrix products, arithmetic and copies ran while one was open for 8% -> 0% of each run, Pallas kernels for 0% -> 0%
where the time goes in v2:
time: 109 us
  Pallas kernels  102 us (94%)
  local copies, waits for them, and re-layouts  6.28 us (6%)
  between operations  1.3 us (1%)
    pallas_call x1, Pallas kernels, local(): pl.pallas_call(functools.partial(kernel, clip_bound, tokens_all), out_sha...  102 us
    unnamed x7, local copies, waits for them, and re-layouts  6.28 us

profile of v2, /device:TPU:0, one launch (start us, length us, event | category | flops | bytes accessed | tf_op | source)
XLA Modules:
  0.0 109.1 jit_solution(247571558528468827)
XLA Ops:
  1.3 101.5 %step.1 = (f32[256,1920]{1,0:T(8,128)}, f32[256,1920]{1,0:T(8,128)}, bf16[384,1920]{1,0:T(8,128)(2,1)}) custom-call(s32[1]{0:T(128)S(6)} %copy.14.newest, f32[8]{0:T(128)} %band.1, f32[256,1920]{1,0:T(8,128)} %weight.1, f32[7,256,1920]{2,1,0:T(8,128)} %history.1, bf16[256,1920]{1,0:T(8,128)(2,1)} %fresh.1, bf16[128,256]{1,0:T(8,128)(2,1)} %x_grad.1, ...), custom_call_target="tpu_custom_call" | custom-call | tf_op jit(solution)/shard_map/step/pallas_call | solution.py:299
  102.8 0.0 copy-start
  102.8 3.1 %copy.15 = f32[256,1920]{1,0:T(8,128)} copy(f32[256,1920]{1,0:T(8,128)} %get-tuple-element.6) | data formatting | bytes 3932160
  105.9 0.0 copy-done
  105.9 0.0 copy-start.1
  105.9 1.3 %copy.16 = f32[256,1920]{1,0:T(8,128)} copy(f32[256,1920]{1,0:T(8,128)S(1)} %copy-done) | data formatting | bytes 3932160
  107.2 0.8 copy-done.1
  108.0 1.1 %copy.17 = bf16[384,1920]{1,0:T(8,128)(2,1)} copy(bf16[384,1920]{1,0:T(8,128)(2,1)S(1)} %copy-done.1) | data formatting | bytes 2949120
Async XLA Ops:
  102.8 3.1 %copy-start = (f32[256,1920]{1,0:T(8,128)S(1)}, f32[256,1920]{1,0:T(8,128)}, u32[]{:S(2)}) copy-start(f32[256,1920]{1,0:T(8,128)} %get-tuple-element.7) | copy-start | bytes 5898244
  105.9 2.1 %copy-start.1 = (bf16[384,1920]{1,0:T(8,128)(2,1)S(1)}, bf16[384,1920]{1,0:T(8,128)(2,1)}, u32[]{:S(2)}) copy-start(bf16[384,1920]{1,0:T(8,128)(2,1)} %get-tuple-element.8) | copy-start | bytes 4423684

commit v3 on v2

--- a/solution.py
+++ b/solution.py
@@ -13,10 +13,12 @@
 noise_multiplier = 0.01
 
 LANES = 128
-ROWS_IN = 224
+ROWS_IN = 256
 PIECES = 4
-LAG_B, LAG_C, LAG_D, LAG_E, LAG_F = 1, 3, 4, 6, 8
-EARLY = 5
+ROWS_FIRST = 64
+LAG_B, LAG_C, LAG_D, LAG_E, LAG_F = 1, 3, 5, 7, 10
+AHEAD = 5
+SEMS = 24
 MESH = pl.DeviceIdType.MESH
 
 
@@ -28,8 +30,8 @@
     clip_bound, tokens_all,
     newest, band, weight, history, fresh, x_grad, dy_grad, x_next,
     new_weight, noise_now, next_out,
-    hist, wv, fr, dyb, wb, xo, xp, psend, precv, own, obuf, xg, dyq, cts, sbuf, rbuf,
-    s_hist, s_wv, s_fr, s_dyr, s_dyf, s_left, s_right, s_opp, s_sib, s_part, s_stat_s, s_stat_r, s_misc,
+    hist, wv, fr, dyb, wb, xo, xp, psend, precv, own, obuf, xg, dyq, raw, cts, sbuf, rbuf, frow,
+    s_hist, s_wv, s_fr, s_dyr, s_dyf, s_left, s_right, s_opp, s_sib, s_part, s_stat, s_misc,
 ):
     chunks = hist.shape[0]
     slots = hist.shape[1]
@@ -47,14 +49,16 @@
     sibling = at(lo, x, oc)
     right, left = at(lo, xr, c), at(lo, xl, c)
     inner = at(1 - lo, x, c)
+    opposite = at(lo, xx, c)
+    cross = at(1 - lo, x, oc)
     flipped = (1 - lo) * 8 + x * 2 + c
     outer = ((1 - hi) * 4 + y, flipped)
     same_hi = [(hi * 4 + (y + s) % 4, f) for s in (1, 3, 2)]
     other_hi = [((1 - hi) * 4 + (y + s) % 4, flipped) for s in (0, 1, 3, 2)]
     other_hi_same_f = [((1 - hi) * 4 + (y + s) % 4, f) for s in (0, 1, 3, 2)]
 
-    (S_XG, S_DYQ, S_XO, S_XIN, S_XOUT, S_CT, S_DYS, S_DYFS, S_W1, S_W2, S_W3, S_PS, S_XS1, S_XS2, S_CTS,
-     S_ONW, S_ONN, S_OUT) = range(18)
+    (S_XG, S_DYQ, S_XO, S_XIN, S_XIN2, S_XOUT, S_CT, S_FR, S_DYS, S_DYFS, S_W1, S_W2, S_W3, S_PS, S_XS1, S_XS2, S_XS3,
+     S_CTS, S_FRS, S_ST1, S_ST2, S_ONW, S_ONN, S_OUT) = range(SEMS)
 
     def cols(k):
         return pl.ds(pl.multiple_of(k * LANES, LANES), LANES)
@@ -63,7 +67,7 @@
         pltpu.make_async_remote_copy(src, dst, send, recv, device_id=to, device_id_type=MESH).start()
 
     barrier = pltpu.get_barrier_semaphore()
-    peers = [sibling, right, left, inner] + same_hi + other_hi_same_f + other_hi
+    peers = other_hi_same_f[::-1] + other_hi[::-1] + same_hi[::-1] + [opposite, cross, inner, right, left, sibling]
     for peer in peers:
         pl.semaphore_signal(barrier, inc=1, device_id=peer, device_id_type=MESH)
 
@@ -84,10 +88,12 @@
         column = pl.ds(pl.multiple_of(d * units + k * LANES, LANES), LANES)
         pltpu.make_async_copy(dy_grad.at[my_rows, column], dyb.at[k, d, c], s_dyr.at[k]).start()
 
-    @pl.loop(0, 2)
+    @pl.loop(0, chunks)
     def _(k):
         fetch_dy(k)
         fetch(k)
+
+    pltpu.make_async_copy(x_next.at[:, pl.ds(pl.multiple_of(lo * half, LANES), half)], xo, s_misc.at[S_XO]).start()
 
     wait_for(xg, s_misc.at[S_XG])
     x_t = xg[...].astype(jnp.float32).T
@@ -100,79 +106,65 @@
     output_part = 0.5 * jnp.sum(total.T, axis=0, keepdims=True)
     row = lax.broadcasted_iota(jnp.int32, (8, LANES), 0)
     sbuf[0] = jnp.where(row == 0, feature_part, jnp.where(row == 1, output_part, 0.0))
+    mine = pl.ds(pl.multiple_of(d * LANES, LANES), LANES)
+    raw[:, mine] = x_t.astype(jnp.bfloat16)
 
     pl.semaphore_wait(barrier, len(peers))
 
-    def stat_send(r, to):
-        remote(sbuf.at[r], rbuf.at[r], s_stat_s.at[r], s_stat_r.at[r], to)
-
-    def stat_take(r):
-        wait_for(rbuf.at[r], s_stat_r.at[r])
-        sbuf[r + 1] = sbuf[r] + rbuf[r]
-
-    def send_dy_to(k, to):
-        column = pl.ds(pl.multiple_of(to[0] * units + k * LANES, LANES), LANES)
-        remote(dy_grad.at[my_rows, column], dyb.at[k, d, c], s_misc.at[S_DYS], s_dyr.at[k], to)
+    for r, to in enumerate((right, opposite, left)):
+        remote(sbuf.at[0], rbuf.at[r], s_misc.at[S_ST1], s_stat.at[r], to)
+    for to in other_hi_same_f[::-1] + same_hi[::-1]:
+        remote(raw.at[:, mine], raw.at[:, mine], s_misc.at[S_CTS], s_misc.at[S_CT], to)
 
     def send_dy(k):
         for to in other_hi + same_hi:
-            send_dy_to(k, to)
-
-    stat_send(0, sibling)
-    send_dy(0)
-    stat_take(0)
-    stat_send(1, at(lo, x + 1 - 2 * (x % 2), c))
+            column = pl.ds(pl.multiple_of(to[0] * units + k * LANES, LANES), LANES)
+            remote(dy_grad.at[my_rows, column], dyb.at[k, d, c], s_misc.at[S_DYS], s_dyr.at[k], to)
+
     other_half = pl.multiple_of((1 - lo) * half, LANES)
-    remote(
-        x_next.at[0:ROWS_IN, pl.ds(other_half, half)], xp.at[0:ROWS_IN], s_misc.at[S_XS1], s_misc.at[S_XIN], inner
-    )
-    send_dy(1)
-    stat_take(1)
-    stat_send(2, at(lo, 3 - x, c))
     width = half // PIECES
 
-    def send_piece(q):
+    def send_inner(low, high, send, recv):
+        remote(
+            x_next.at[low:high, pl.ds(other_half, half)], xp.at[low:high], s_misc.at[send], s_misc.at[recv], inner
+        )
+
+    def send_outer(q):
         remote(
             x_next.at[ROWS_IN:, pl.ds(pl.multiple_of(other_half + q * width, LANES), width)],
             xp.at[ROWS_IN:, pl.ds(pl.multiple_of(q * width, LANES), width)],
             s_misc.at[S_XS2], s_misc.at[S_XOUT], outer,
         )
 
-    stat_take(2)
-    stat_send(3, inner)
-
-    @pl.loop(2, EARLY)
-    def _(k):
+    for r in range(3):
+        wait_for(rbuf.at[r], s_stat.at[r])
+    sbuf[1] = (sbuf[0] + rbuf[0]) + (rbuf[1] + rbuf[2])
+    for r, to in enumerate((sibling, inner, cross)):
+        remote(sbuf.at[1], rbuf.at[3 + r], s_misc.at[S_ST2], s_stat.at[3 + r], to)
+    send_dy(0)
+    send_inner(0, ROWS_FIRST, S_XS1, S_XIN)
+    for r in range(3, 6):
+        wait_for(rbuf.at[r], s_stat.at[r])
+    both = (sbuf[1] + rbuf[3]) + (rbuf[4] + rbuf[5])
+    frow[d] = jnp.minimum(1.0, clip_bound / jnp.sqrt(both[0:1] * both[1:2] + eps_value))
+    for to in other_hi_same_f[::-1] + same_hi[::-1]:
+        remote(frow.at[d], frow.at[d], s_misc.at[S_FRS], s_misc.at[S_FR], to)
+
+    send_inner(ROWS_FIRST, ROWS_IN, S_XS3, S_XIN2)
+    for k in range(1, AHEAD):
+        if k <= PIECES:
+            send_outer(k - 1)
         send_dy(k)
-        send_piece(k - 2)
-
-    stat_take(3)
-    both = sbuf[4]
-    factor = jnp.minimum(1.0, clip_bound / jnp.sqrt(both[0:1] * both[1:2] + eps_value))
-    mine = pl.ds(pl.multiple_of(d * LANES, LANES), LANES)
-    cts[:, mine] = (x_t * factor).astype(jnp.bfloat16)
-    for to in other_hi_same_f + same_hi:
-        remote(cts.at[:, mine], cts.at[:, mine], s_misc.at[S_CTS], s_misc.at[S_CT], to)
-
-    for q in range(EARLY - 2, PIECES):
-        send_piece(q)
-
-    @pl.loop(EARLY, chunks)
-    def _(k):
-        send_dy(k)
-
-    pltpu.make_async_copy(x_next.at[:, pl.ds(pl.multiple_of(lo * half, LANES), half)], xo, s_misc.at[S_XO]).start()
-
-    @pl.loop(2, chunks)
-    def _(k):
-        fetch_dy(k)
-        fetch(k)
 
     first = newest[0]
     mixing = [band[lax.rem(first + (slots - s), slots) + 1] for s in range(slots)]
     now_coefficient = band[0]
 
-    wait_for(cts.at[:, 0 : 7 * LANES], s_misc.at[S_CT])
+    wait_for(raw.at[:, 0 : 7 * LANES], s_misc.at[S_CT])
+    wait_for(frow.at[0:7], s_misc.at[S_FR])
+    for n in range(8):
+        block = slice(n * LANES, (n + 1) * LANES)
+        cts[:, block] = (raw[:, block].astype(jnp.float32) * frow[n]).astype(jnp.bfloat16)
 
     def stage_a(k):
         wait_for(dyb.at[k, :, c], s_dyr.at[k])
@@ -232,7 +224,8 @@
         @pl.when(k == 0)
         def _():
             wait_for(xo, s_misc.at[S_XO])
-            wait_for(xp.at[0:ROWS_IN], s_misc.at[S_XIN])
+            wait_for(xp.at[0:ROWS_FIRST], s_misc.at[S_XIN])
+            wait_for(xp.at[ROWS_FIRST:ROWS_IN], s_misc.at[S_XIN2])
             wait_for(xp.at[ROWS_IN:], s_misc.at[S_XOUT])
 
         wait_for(wb.at[k, :, oc], s_sib.at[k])
@@ -261,6 +254,7 @@
 
     @pl.loop(0, chunks + LAG_F)
     def _(t):
+        staged(send_dy, t + AHEAD, 0)
         staged(stage_c, t, LAG_C)
         staged(stage_d, t, LAG_D)
         staged(stage_a, t, 0)
@@ -268,13 +262,15 @@
         staged(stage_e, t, LAG_E)
         staged(stage_f, t, LAG_F)
 
-    for r in range(4):
-        wait_for(sbuf.at[r], s_stat_s.at[r])
+    wait_for(rbuf.at[0:3], s_misc.at[S_ST1])
+    wait_for(rbuf.at[0:3], s_misc.at[S_ST2])
+    wait_for(frow.at[0:7], s_misc.at[S_FRS])
     wait_for(dyb.at[:, 0:7, 0], s_misc.at[S_DYS])
     wait_for(dyb.at[:, :, 0], s_misc.at[S_DYFS])
-    wait_for(xp.at[0:ROWS_IN], s_misc.at[S_XS1])
+    wait_for(xp.at[0:ROWS_FIRST], s_misc.at[S_XS1])
+    wait_for(xp.at[ROWS_FIRST:ROWS_IN], s_misc.at[S_XS3])
     wait_for(xp.at[ROWS_IN:], s_misc.at[S_XS2])
-    wait_for(cts.at[:, 0 : 7 * LANES], s_misc.at[S_CTS])
+    wait_for(raw.at[:, 0 : 7 * LANES], s_misc.at[S_CTS])
     wait_for(wb.at[:, 0:3, 0], s_misc.at[S_W1])
     wait_for(wb.at[:, 0, 0], s_misc.at[S_W2])
     wait_for(wb.at[:, 0:3, 0], s_misc.at[S_W3])
@@ -320,13 +316,15 @@
             pltpu.VMEM(x_grad.shape, b16),
             pltpu.VMEM((x_grad.shape[0], units), b16),
             pltpu.VMEM((rows, tokens_all), b16),
-            pltpu.VMEM((5, 8, LANES), f32),
-            pltpu.VMEM((4, 8, LANES), f32),
+            pltpu.VMEM((rows, tokens_all), b16),
+            pltpu.VMEM((2, 8, LANES), f32),
+            pltpu.VMEM((6, 8, LANES), f32),
+            pltpu.VMEM((8, 1, LANES), f32),
         ]
         + [per_chunk] * 10
-        + [pltpu.SemaphoreType.DMA((4,)), pltpu.SemaphoreType.DMA((4,)), pltpu.SemaphoreType.DMA((18,))],
+        + [pltpu.SemaphoreType.DMA((6,)), pltpu.SemaphoreType.DMA((SEMS,))],
         compiler_params=pltpu.CompilerParams(
-            collective_id=0, has_side_effects=True, vmem_limit_bytes=67043328
+            collective_id=0, has_side_effects=True, vmem_limit_bytes=45 * 2**20
         ),
         name="step",
     )(newest, band, weight, history, fresh, x_grad, dy_grad, x_next)

time: 109 us -> 95.2 us (0.87)
  Pallas kernels: 102 us -> 85.4 us
  local copies, waits for them, and re-layouts: 6.28 us -> 7.89 us
    pallas_call x1, Pallas kernels: 102 us -> 85.4 us  [local(): pl.pallas_call(functools.partial(kernel, clip_bound, tokens_all), out_sha...]
    unnamed x7 -> x11, local copies, waits for them, and re-layouts: 6.28 us -> 7.89 us
where the time goes in v3:
time: 95.2 us; the launch traced here: 94.6 us
  Pallas kernels  85.4 us (90%)
  local copies, waits for them, and re-layouts  7.89 us (8%)
  between operations  1.3 us (1%)
    pallas_call x1, Pallas kernels, local(): pl.pallas_call(functools.partial(kernel, clip_bound, tokens_all), out_sha...  85.4 us
    unnamed x11, local copies, waits for them, and re-layouts  7.89 us

profile of v3, /device:TPU:0, one launch (start us, length us, event | category | flops | bytes accessed | tf_op | source)
XLA Modules:
  0.0 94.6 jit_solution(12451276880590739778)
XLA Ops:
  1.3 0.0 copy-start
  1.3 1.5 %copy-done = f32[256,1920]{1,0:T(8,128)S(1)} copy-done((f32[256,1920]{1,0:T(8,128)S(1)}, f32[256,1920]{1,0:T(8,128)}, u32[]{:S(2)}) %copy-start) | copy-done | bytes 1966104
  2.8 0.0 copy-start.1
  2.8 1.2 %copy-done.1 = bf16[256,1920]{1,0:T(8,128)(2,1)S(1)} copy-done((bf16[256,1920]{1,0:T(8,128)(2,1)S(1)}, bf16[256,1920]{1,0:T(8,128)(2,1)}, u32[]{:S(2)}) %copy-start.1) | copy-done | bytes 983064
  4.0 0.0 copy-start.2
  4.0 0.8 copy-done.2
  4.9 0.0 copy-start.3
  4.9 0.7 copy-done.3
  5.5 85.4 %step.1 = (f32[256,1920]{1,0:T(8,128)S(1)}, f32[256,1920]{1,0:T(8,128)S(1)}, bf16[384,1920]{1,0:T(8,128)(2,1)S(1)}) custom-call(s32[1]{0:T(128)S(6)} %copy.14.newest, f32[8]{0:T(128)S(1)} %copy-done.3, f32[256,1920]{1,0:T(8,128)S(1)} %copy-done, f32[7,256,1920]{2,1,0:T(8,128)} %history.1, bf16[256,1920]{1,0:T(8,128)(2,1)S(1)} %copy-done.1, ...), custom_call_target="tpu_custom_call" | custom-call | tf_op jit(solution)/shard_map/step/pallas_call | solution.py:295
  90.9 1.3 %copy.15 = f32[256,1920]{1,0:T(8,128)} copy(f32[256,1920]{1,0:T(8,128)S(1)} %get-tuple-element.6) | data formatting | bytes 3932160
  92.2 1.3 %copy.16 = f32[256,1920]{1,0:T(8,128)} copy(f32[256,1920]{1,0:T(8,128)S(1)} %get-tuple-element.7) | data formatting | bytes 3932160
  93.5 1.1 %copy.17 = bf16[384,1920]{1,0:T(8,128)(2,1)} copy(bf16[384,1920]{1,0:T(8,128)(2,1)S(1)} %get-tuple-element.8) | data formatting | bytes 2949120
Async XLA Ops:
  1.3 1.5 %copy-start = (f32[256,1920]{1,0:T(8,128)S(1)}, f32[256,1920]{1,0:T(8,128)}, u32[]{:S(2)}) copy-start(f32[256,1920]{1,0:T(8,128)} %weight.1) | copy-start | bytes 5898244
  2.8 1.2 %copy-start.1 = (bf16[256,1920]{1,0:T(8,128)(2,1)S(1)}, bf16[256,1920]{1,0:T(8,128)(2,1)}, u32[]{:S(2)}) copy-start(bf16[256,1920]{1,0:T(8,128)(2,1)} %fresh.1) | copy-start | bytes 2949124
  4.0 0.8 copy-start.2
  4.9 0.7 copy-start.3

commit v4 on v3

--- a/solution.py
+++ b/solution.py
@@ -13,12 +13,12 @@
 noise_multiplier = 0.01
 
 LANES = 128
-ROWS_IN = 256
-PIECES = 4
-ROWS_FIRST = 64
-LAG_B, LAG_C, LAG_D, LAG_E, LAG_F = 1, 3, 5, 7, 10
-AHEAD = 5
-SEMS = 24
+ROWS_IN = 240
+ROWS_FIRST = 32
+SPECIAL = 4
+LAG_A, LAG_B, LAG_C, LAG_D, LAG_E = 6, 10, 2, 4, 6
+ROUND, RELAY, SUM, PASS, LAST = 1, 7, 13, 15, 17
+SEMS = 28
 MESH = pl.DeviceIdType.MESH
 
 
@@ -30,8 +30,8 @@
     clip_bound, tokens_all,
     newest, band, weight, history, fresh, x_grad, dy_grad, x_next,
     new_weight, noise_now, next_out,
-    hist, wv, fr, dyb, wb, xo, xp, psend, precv, own, obuf, xg, dyq, raw, cts, sbuf, rbuf, frow,
-    s_hist, s_wv, s_fr, s_dyr, s_dyf, s_left, s_right, s_opp, s_sib, s_part, s_stat, s_misc,
+    hist, wv, fr, dyb, wb, xo, xp, psend, precv, own, obuf, xg, dyq, cts, sall, sbuf, rbuf,
+    s_hist, s_wv, s_fr, s_dyr, s_dyf, s_left, s_right, s_opp, s_sib, s_part, s_stat, s_onn, s_misc,
 ):
     chunks = hist.shape[0]
     slots = hist.shape[1]
@@ -55,10 +55,11 @@
     outer = ((1 - hi) * 4 + y, flipped)
     same_hi = [(hi * 4 + (y + s) % 4, f) for s in (1, 3, 2)]
     other_hi = [((1 - hi) * 4 + (y + s) % 4, flipped) for s in (0, 1, 3, 2)]
-    other_hi_same_f = [((1 - hi) * 4 + (y + s) % 4, f) for s in (0, 1, 3, 2)]
-
-    (S_XG, S_DYQ, S_XO, S_XIN, S_XIN2, S_XOUT, S_CT, S_FR, S_DYS, S_DYFS, S_W1, S_W2, S_W3, S_PS, S_XS1, S_XS2, S_XS3,
-     S_CTS, S_FRS, S_ST1, S_ST2, S_ONW, S_ONN, S_OUT) = range(SEMS)
+    d_far = (1 - hi) * 4 + y
+    far = (d_far, f)
+
+    (S_XG, S_DYQ, S_XO, S_XIN, S_XIN2, S_XOUT, S_CTY, S_CTZ, S_CTR, S_SY, S_SZ, S_SR, S_DYS, S_DYFS, S_W1, S_W2, S_W3,
+     S_PS, S_XS1, S_XS2, S_XS3, S_CTS, S_CTRS, S_SS, S_SRS, S_ST, S_ONW, S_OUT) = range(SEMS)
 
     def cols(k):
         return pl.ds(pl.multiple_of(k * LANES, LANES), LANES)
@@ -67,7 +68,7 @@
         pltpu.make_async_remote_copy(src, dst, send, recv, device_id=to, device_id_type=MESH).start()
 
     barrier = pltpu.get_barrier_semaphore()
-    peers = other_hi_same_f[::-1] + other_hi[::-1] + same_hi[::-1] + [opposite, cross, inner, right, left, sibling]
+    peers = [far] + other_hi[::-1] + same_hi[::-1] + [opposite, cross, inner, right, left, sibling]
     for peer in peers:
         pl.semaphore_signal(barrier, inc=1, device_id=peer, device_id_type=MESH)
 
@@ -107,14 +108,11 @@
     row = lax.broadcasted_iota(jnp.int32, (8, LANES), 0)
     sbuf[0] = jnp.where(row == 0, feature_part, jnp.where(row == 1, output_part, 0.0))
     mine = pl.ds(pl.multiple_of(d * LANES, LANES), LANES)
-    raw[:, mine] = x_t.astype(jnp.bfloat16)
 
     pl.semaphore_wait(barrier, len(peers))
 
     for r, to in enumerate((right, opposite, left)):
-        remote(sbuf.at[0], rbuf.at[r], s_misc.at[S_ST1], s_stat.at[r], to)
-    for to in other_hi_same_f[::-1] + same_hi[::-1]:
-        remote(raw.at[:, mine], raw.at[:, mine], s_misc.at[S_CTS], s_misc.at[S_CT], to)
+        remote(sbuf.at[0], rbuf.at[r], s_misc.at[S_ST], s_stat.at[r], to)
 
     def send_dy(k):
         for to in other_hi + same_hi:
@@ -122,73 +120,95 @@
             remote(dy_grad.at[my_rows, column], dyb.at[k, d, c], s_misc.at[S_DYS], s_dyr.at[k], to)
 
     other_half = pl.multiple_of((1 - lo) * half, LANES)
-    width = half // PIECES
-
-    def send_inner(low, high, send, recv):
-        remote(
-            x_next.at[low:high, pl.ds(other_half, half)], xp.at[low:high], s_misc.at[send], s_misc.at[recv], inner
-        )
-
-    def send_outer(q):
-        remote(
-            x_next.at[ROWS_IN:, pl.ds(pl.multiple_of(other_half + q * width, LANES), width)],
-            xp.at[ROWS_IN:, pl.ds(pl.multiple_of(q * width, LANES), width)],
-            s_misc.at[S_XS2], s_misc.at[S_XOUT], outer,
-        )
-
-    for r in range(3):
-        wait_for(rbuf.at[r], s_stat.at[r])
-    sbuf[1] = (sbuf[0] + rbuf[0]) + (rbuf[1] + rbuf[2])
-    for r, to in enumerate((sibling, inner, cross)):
-        remote(sbuf.at[1], rbuf.at[3 + r], s_misc.at[S_ST2], s_stat.at[3 + r], to)
-    send_dy(0)
-    send_inner(0, ROWS_FIRST, S_XS1, S_XIN)
-    for r in range(3, 6):
-        wait_for(rbuf.at[r], s_stat.at[r])
-    both = (sbuf[1] + rbuf[3]) + (rbuf[4] + rbuf[5])
-    frow[d] = jnp.minimum(1.0, clip_bound / jnp.sqrt(both[0:1] * both[1:2] + eps_value))
-    for to in other_hi_same_f[::-1] + same_hi[::-1]:
-        remote(frow.at[d], frow.at[d], s_misc.at[S_FRS], s_misc.at[S_FR], to)
-
-    send_inner(ROWS_FIRST, ROWS_IN, S_XS3, S_XIN2)
-    for k in range(1, AHEAD):
-        if k <= PIECES:
-            send_outer(k - 1)
-        send_dy(k)
+
+    def send_tokens(low, high, send, recv, to):
+        remote(x_next.at[low:high, pl.ds(other_half, half)], xp.at[low:high], s_misc.at[send], s_misc.at[recv], to)
+
+    all_rows = xp.shape[0]
+    send_tokens(ROWS_IN, all_rows, S_XS2, S_XOUT, outer)
+    send_tokens(0, ROWS_FIRST, S_XS1, S_XIN, inner)
 
     first = newest[0]
     mixing = [band[lax.rem(first + (slots - s), slots) + 1] for s in range(slots)]
     now_coefficient = band[0]
 
-    wait_for(raw.at[:, 0 : 7 * LANES], s_misc.at[S_CT])
-    wait_for(frow.at[0:7], s_misc.at[S_FR])
-    for n in range(8):
-        block = slice(n * LANES, (n + 1) * LANES)
-        cts[:, block] = (raw[:, block].astype(jnp.float32) * frow[n]).astype(jnp.bfloat16)
+    rate = learn_rate / tokens_all
+
+    def column_of(slot):
+        return slot - (slot + 15 - SPECIAL) // 16
+
+    def slot_of(k):
+        return k + (k + 16 - SPECIAL) // 16
+
+    def second_round():
+        for r in range(3):
+            wait_for(rbuf.at[r], s_stat.at[r])
+        sbuf[1] = (sbuf[0] + rbuf[0]) + (rbuf[1] + rbuf[2])
+        for r, to in enumerate((sibling, inner, cross)):
+            remote(sbuf.at[1], rbuf.at[3 + r], s_misc.at[S_ST], s_stat.at[3 + r], to)
+        send_tokens(ROWS_FIRST, ROWS_IN, S_XS3, S_XIN2, inner)
+
+    def clip_rows():
+        for r in range(3, 6):
+            wait_for(rbuf.at[r], s_stat.at[r])
+        both = (sbuf[1] + rbuf[3]) + (rbuf[4] + rbuf[5])
+        factor = jnp.minimum(1.0, clip_bound / jnp.sqrt(both[0:1] * both[1:2] + eps_value))
+        clipped = (xg[...].astype(jnp.float32).T * factor).astype(jnp.bfloat16)
+        cts[:, mine] = clipped
+        wb[SPECIAL, x, c] = clipped
+        for to in same_hi:
+            remote(cts.at[:, mine], cts.at[:, mine], s_misc.at[S_CTS], s_misc.at[S_CTY], to)
+        remote(cts.at[:, mine], cts.at[:, mine], s_misc.at[S_CTS], s_misc.at[S_CTZ], far)
+
+    theirs_far = pl.ds(pl.multiple_of(d_far * LANES, LANES), LANES)
+
+    def pass_on(ref, arrived, send, recv):
+        block = ref.at[:, theirs_far]
+        wait_for(block, s_misc.at[arrived])
+        for to in same_hi:
+            remote(block, block, s_misc.at[send], s_misc.at[recv], to)
+
+    three = pl.ds(0, 3 * LANES)
 
     def stage_a(k):
         wait_for(dyb.at[k, :, c], s_dyr.at[k])
         remote(dyb.at[k, :, c], dyb.at[k, :, c], s_misc.at[S_DYFS], s_dyf.at[k], sibling)
 
+    def stage_ring(slot):
+        @pl.when(slot != SPECIAL)
+        def _():
+            k = column_of(slot)
+            wait_for(hist.at[k], s_hist.at[k])
+            wait_for(wv.at[k], s_wv.at[k])
+            wait_for(fr.at[k], s_fr.at[k])
+            combined = mixing[0] * hist[k, 0]
+            for s in range(1, slots):
+                combined = combined + mixing[s] * hist[k, s]
+            noise = (fr[k].astype(jnp.float32) - combined) / jnp.full(combined.shape, now_coefficient, jnp.float32)
+            hist[k, 0] = noise
+            base = wv[k] - (rate * (noise_multiplier * clip_bound)) * noise
+            wb[slot, x, c] = base.astype(jnp.bfloat16)
+            wv[k] = base
+            pltpu.make_async_copy(hist.at[k, 0], noise_now.at[:, cols(k)], s_onn).start()
+
+        @pl.when(slot == SPECIAL)
+        def _():
+            clip_rows()
+
+        block = wb.at[slot, x, c]
+        remote(block, block, s_misc.at[S_W1], s_left.at[slot], right)
+        remote(block, block, s_misc.at[S_W1], s_right.at[slot], left)
+        remote(block, block, s_misc.at[S_W1], s_sib.at[slot], sibling)
+
     def stage_b(k):
-        wait_for(hist.at[k], s_hist.at[k])
-        wait_for(wv.at[k], s_wv.at[k])
-        wait_for(fr.at[k], s_fr.at[k])
-        combined = mixing[0] * hist[k, 0]
-        for s in range(1, slots):
-            combined = combined + mixing[s] * hist[k, s]
-        noise = (fr[k].astype(jnp.float32) - combined) / jnp.full(combined.shape, now_coefficient, jnp.float32)
-        hist[k, 0] = noise
+        @pl.when(k == 0)
+        def _():
+            wait_for(cts.at[:, three], s_misc.at[S_CTY])
+            wait_for(cts.at[:, three], s_misc.at[S_CTR])
+
         wait_for(dyb.at[k, :, oc], s_dyf.at[k])
         gradient = jnp.dot(cts[...], dyb[k].reshape(8 * LANES, LANES), preferred_element_type=jnp.float32)
-        updated = wv[k] - learn_rate * (gradient + (noise_multiplier * clip_bound) * noise) * (1.0 / tokens_all)
-        wb[k, x, c] = updated.astype(jnp.bfloat16)
-        wv[k] = updated
-        block = wb.at[k, x, c]
-        remote(block, block, s_misc.at[S_W1], s_left.at[k], right)
-        remote(block, block, s_misc.at[S_W1], s_right.at[k], left)
-        remote(block, block, s_misc.at[S_W1], s_sib.at[k], sibling)
-        pltpu.make_async_copy(hist.at[k, 0], noise_now.at[:, cols(k)], s_misc.at[S_ONN]).start()
+        wv[k] = wv[k] - rate * gradient
         pltpu.make_async_copy(wv.at[k], new_weight.at[:, cols(k)], s_misc.at[S_ONW]).start()
 
     upper, lower = pl.ds(0, LANES), pl.ds(LANES, LANES)
@@ -234,48 +254,68 @@
         def _():
             multiply((k - 1, k))
 
-        if chunks % 2 == 1:
-
-            @pl.when(k == chunks - 1)
-            def _():
-                multiply((k,))
+    def sum_special():
+        wait_for(precv.at[SPECIAL], s_part.at[SPECIAL])
+        sall[:, mine] = (own[SPECIAL] + precv[SPECIAL].astype(jnp.float32)).astype(jnp.bfloat16)
+        for to in same_hi:
+            remote(sall.at[:, mine], sall.at[:, mine], s_misc.at[S_SS], s_misc.at[S_SY], to)
+        remote(sall.at[:, mine], sall.at[:, mine], s_misc.at[S_SS], s_misc.at[S_SZ], far)
 
     def stage_f(k):
-        wait_for(precv.at[k], s_part.at[k])
-        obuf[k] = (own[k] + precv[k].astype(jnp.float32)).astype(jnp.bfloat16)
+        @pl.when(k == 0)
+        def _():
+            wait_for(sall.at[:, three], s_misc.at[S_SY])
+            wait_for(sall.at[:, three], s_misc.at[S_SR])
+
+        slot = slot_of(k)
+        moved = jnp.dot(sall[...], dyb[k].reshape(8 * LANES, LANES), preferred_element_type=jnp.float32)
+        wait_for(precv.at[slot], s_part.at[slot])
+        obuf[k] = (own[slot] + precv[slot].astype(jnp.float32) - rate * moved).astype(jnp.bfloat16)
         pltpu.make_async_copy(obuf.at[k], next_out.at[:, cols(k)], s_misc.at[S_OUT]).start()
 
-    def staged(stage, t, lag):
-        k = t - lag
-
-        @pl.when((k >= 0) & (k < chunks))
+    ring = wb.shape[0]
+
+    def staged(stage, k, count):
+        @pl.when((k >= 0) & (k < count))
         def _():
             stage(k)
 
-    @pl.loop(0, chunks + LAG_F)
+    def once(t, step, action):
+        @pl.when(t == step)
+        def _():
+            action()
+
+    @pl.loop(0, LAST + (chunks + 1) // 2)
     def _(t):
-        staged(send_dy, t + AHEAD, 0)
-        staged(stage_c, t, LAG_C)
-        staged(stage_d, t, LAG_D)
-        staged(stage_a, t, 0)
-        staged(stage_b, t, LAG_B)
-        staged(stage_e, t, LAG_E)
-        staged(stage_f, t, LAG_F)
-
-    wait_for(rbuf.at[0:3], s_misc.at[S_ST1])
-    wait_for(rbuf.at[0:3], s_misc.at[S_ST2])
-    wait_for(frow.at[0:7], s_misc.at[S_FRS])
+        once(t, ROUND, second_round)
+        staged(stage_c, t - LAG_C, ring)
+        staged(stage_d, t - LAG_D, ring)
+        staged(stage_ring, t, ring)
+        staged(send_dy, t, chunks)
+        once(t, RELAY, lambda: pass_on(cts, S_CTZ, S_CTRS, S_CTR))
+        once(t, SUM, sum_special)
+        once(t, PASS, lambda: pass_on(sall, S_SZ, S_SRS, S_SR))
+        staged(stage_e, t - LAG_E, ring)
+        staged(stage_a, t - LAG_A, chunks)
+        staged(stage_b, t - LAG_B, chunks)
+        staged(stage_f, 2 * (t - LAST), chunks)
+        staged(stage_f, 2 * (t - LAST) + 1, chunks)
+
+    wait_for(rbuf, s_misc.at[S_ST])
     wait_for(dyb.at[:, 0:7, 0], s_misc.at[S_DYS])
     wait_for(dyb.at[:, :, 0], s_misc.at[S_DYFS])
     wait_for(xp.at[0:ROWS_FIRST], s_misc.at[S_XS1])
     wait_for(xp.at[ROWS_FIRST:ROWS_IN], s_misc.at[S_XS3])
     wait_for(xp.at[ROWS_IN:], s_misc.at[S_XS2])
-    wait_for(raw.at[:, 0 : 7 * LANES], s_misc.at[S_CTS])
+    wait_for(cts.at[:, 0 : 4 * LANES], s_misc.at[S_CTS])
+    wait_for(cts.at[:, three], s_misc.at[S_CTRS])
+    wait_for(sall.at[:, 0 : 4 * LANES], s_misc.at[S_SS])
+    wait_for(sall.at[:, three], s_misc.at[S_SRS])
     wait_for(wb.at[:, 0:3, 0], s_misc.at[S_W1])
     wait_for(wb.at[:, 0, 0], s_misc.at[S_W2])
     wait_for(wb.at[:, 0:3, 0], s_misc.at[S_W3])
     wait_for(psend, s_misc.at[S_PS])
-    wait_for(hist.at[:, 0], s_misc.at[S_ONN])
+    wait_for(hist.at[:, 0], s_onn)
     wait_for(wv, s_misc.at[S_ONW])
     wait_for(obuf, s_misc.at[S_OUT])
 
@@ -306,23 +346,23 @@
             pltpu.VMEM((chunks, rows, LANES), f32),
             pltpu.VMEM((chunks, rows, LANES), b16),
             pltpu.VMEM((chunks, 8, 2, 64, LANES), b16),
-            pltpu.VMEM((chunks, 4, 2, rows, LANES), b16),
+            pltpu.VMEM((chunks + 1, 4, 2, rows, LANES), b16),
             pltpu.VMEM((tokens, half), b16),
             pltpu.VMEM((tokens, half), b16),
-            pltpu.VMEM((chunks, tokens, LANES), b16),
-            pltpu.VMEM((chunks, tokens, LANES), b16),
-            pltpu.VMEM((chunks, tokens, LANES), f32),
+            pltpu.VMEM((chunks + 1, tokens, LANES), b16),
+            pltpu.VMEM((chunks + 1, tokens, LANES), b16),
+            pltpu.VMEM((chunks + 1, tokens, LANES), f32),
             pltpu.VMEM((chunks, tokens, LANES), b16),
             pltpu.VMEM(x_grad.shape, b16),
             pltpu.VMEM((x_grad.shape[0], units), b16),
             pltpu.VMEM((rows, tokens_all), b16),
-            pltpu.VMEM((rows, tokens_all), b16),
+            pltpu.VMEM((tokens, tokens_all), b16),
             pltpu.VMEM((2, 8, LANES), f32),
             pltpu.VMEM((6, 8, LANES), f32),
-            pltpu.VMEM((8, 1, LANES), f32),
         ]
-        + [per_chunk] * 10
-        + [pltpu.SemaphoreType.DMA((6,)), pltpu.SemaphoreType.DMA((SEMS,))],
+        + [per_chunk] * 5
+        + [pltpu.SemaphoreType.DMA((chunks + 1,))] * 5
+        + [pltpu.SemaphoreType.DMA((6,)), pltpu.SemaphoreType.DMA, pltpu.SemaphoreType.DMA((SEMS,))],
         compiler_params=pltpu.CompilerParams(
             collective_id=0, has_side_effects=True, vmem_limit_bytes=45 * 2**20
         ),

time: 95.2 us -> 84.8 us (0.89)
  Pallas kernels: 85.4 us -> 75.3 us
    pallas_call x1, Pallas kernels: 85.4 us -> 75.3 us  [local(): pl.pallas_call(functools.partial(kernel, clip_bound, tokens_all), out_sha...]
where the time goes in v4:
time: 84.8 us; the launch traced here: 84.5 us
  Pallas kernels  75.3 us (89%)
  local copies, waits for them, and re-layouts  7.89 us (9%)
  between operations  1.3 us (2%)
    pallas_call x1, Pallas kernels, local(): pl.pallas_call(functools.partial(kernel, clip_bound, tokens_all), out_sha...  75.3 us
    unnamed x11, local copies, waits for them, and re-layouts  7.89 us

profile of v4, /device:TPU:0, one launch (start us, length us, event | category | flops | bytes accessed | tf_op | source)
XLA Modules:
  0.0 84.5 jit_solution(2042956024493049744)
XLA Ops:
  1.3 0.0 copy-start
  1.3 1.5 %copy-done = f32[256,1920]{1,0:T(8,128)S(1)} copy-done((f32[256,1920]{1,0:T(8,128)S(1)}, f32[256,1920]{1,0:T(8,128)}, u32[]{:S(2)}) %copy-start) | copy-done | bytes 1966104
  2.8 0.0 copy-start.1
  2.8 1.2 %copy-done.1 = bf16[256,1920]{1,0:T(8,128)(2,1)S(1)} copy-done((bf16[256,1920]{1,0:T(8,128)(2,1)S(1)}, bf16[256,1920]{1,0:T(8,128)(2,1)}, u32[]{:S(2)}) %copy-start.1) | copy-done | bytes 983064
  4.0 0.0 copy-start.2
  4.0 0.8 copy-done.2
  4.9 0.0 copy-start.3
  4.9 0.7 copy-done.3
  5.5 75.3 %step.1 = (f32[256,1920]{1,0:T(8,128)S(1)}, f32[256,1920]{1,0:T(8,128)S(1)}, bf16[384,1920]{1,0:T(8,128)(2,1)S(1)}) custom-call(s32[1]{0:T(128)S(6)} %copy.14.newest, f32[8]{0:T(128)S(1)} %copy-done.3, f32[256,1920]{1,0:T(8,128)S(1)} %copy-done, f32[7,256,1920]{2,1,0:T(8,128)} %history.1, bf16[256,1920]{1,0:T(8,128)(2,1)S(1)} %copy-done.1, ...), custom_call_target="tpu_custom_call" | custom-call | tf_op jit(solution)/shard_map/step/pallas_call | solution.py:335
  80.9 1.3 %copy.15 = f32[256,1920]{1,0:T(8,128)} copy(f32[256,1920]{1,0:T(8,128)S(1)} %get-tuple-element.6) | data formatting | bytes 3932160
  82.1 1.3 %copy.16 = f32[256,1920]{1,0:T(8,128)} copy(f32[256,1920]{1,0:T(8,128)S(1)} %get-tuple-element.7) | data formatting | bytes 3932160
  83.4 1.1 %copy.17 = bf16[384,1920]{1,0:T(8,128)(2,1)} copy(bf16[384,1920]{1,0:T(8,128)(2,1)S(1)} %get-tuple-element.8) | data formatting | bytes 2949120
Async XLA Ops:
  1.3 1.5 %copy-start = (f32[256,1920]{1,0:T(8,128)S(1)}, f32[256,1920]{1,0:T(8,128)}, u32[]{:S(2)}) copy-start(f32[256,1920]{1,0:T(8,128)} %weight.1) | copy-start | bytes 5898244
  2.8 1.2 %copy-start.1 = (bf16[256,1920]{1,0:T(8,128)(2,1)S(1)}, bf16[256,1920]{1,0:T(8,128)(2,1)}, u32[]{:S(2)}) copy-start(bf16[256,1920]{1,0:T(8,128)(2,1)} %fresh.1) | copy-start | bytes 2949124
  4.0 0.8 copy-start.2
  4.9 0.7 copy-start.3

commit v5 on v4

--- a/solution.py
+++ b/solution.py
@@ -13,12 +13,14 @@
 noise_multiplier = 0.01
 
 LANES = 128
-ROWS_IN = 240
+ROWS_IN = 144
+ROWS_SHARED = 32
 ROWS_FIRST = 32
 SPECIAL = 4
 LAG_A, LAG_B, LAG_C, LAG_D, LAG_E = 6, 10, 2, 4, 6
-ROUND, RELAY, SUM, PASS, LAST = 1, 7, 13, 15, 17
-SEMS = 28
+SHARE = 3
+ROUND, RELAY, SUM, PASS, LAST = 1, 7, 13, 16, 19
+SEMS = 32
 MESH = pl.DeviceIdType.MESH
 
 
@@ -59,7 +61,8 @@
     far = (d_far, f)
 
     (S_XG, S_DYQ, S_XO, S_XIN, S_XIN2, S_XOUT, S_CTY, S_CTZ, S_CTR, S_SY, S_SZ, S_SR, S_DYS, S_DYFS, S_W1, S_W2, S_W3,
-     S_PS, S_XS1, S_XS2, S_XS3, S_CTS, S_CTRS, S_SS, S_SRS, S_ST, S_ONW, S_OUT) = range(SEMS)
+     S_PS, S_XS1, S_XS2, S_XS3, S_CTS, S_CTRS, S_SS, S_SRS, S_ST, S_ONW, S_OUT,
+     S_XSH, S_XSR, S_XSS, S_XSRS) = range(SEMS)
 
     def cols(k):
         return pl.ds(pl.multiple_of(k * LANES, LANES), LANES)
@@ -125,7 +128,12 @@
         remote(x_next.at[low:high, pl.ds(other_half, half)], xp.at[low:high], s_misc.at[send], s_misc.at[recv], to)
 
     all_rows = xp.shape[0]
-    send_tokens(ROWS_IN, all_rows, S_XS2, S_XOUT, outer)
+    rows_direct = all_rows - 4 * ROWS_SHARED
+    my_share = pl.ds(pl.multiple_of(rows_direct + y * ROWS_SHARED, ROWS_SHARED), ROWS_SHARED)
+    remote(
+        x_next.at[my_share, pl.ds(other_half, half)], xp.at[my_share], s_misc.at[S_XSS], s_misc.at[S_XSH], outer
+    )
+    send_tokens(ROWS_IN, rows_direct, S_XS2, S_XOUT, outer)
     send_tokens(0, ROWS_FIRST, S_XS1, S_XIN, inner)
 
     first = newest[0]
@@ -169,6 +177,12 @@
             remote(block, block, s_misc.at[send], s_misc.at[recv], to)
 
     three = pl.ds(0, 3 * LANES)
+
+    def share_tokens():
+        block = xp.at[my_share]
+        wait_for(block, s_misc.at[S_XSH])
+        for to in same_hi:
+            remote(block, block, s_misc.at[S_XSRS], s_misc.at[S_XSR], to)
 
     def stage_a(k):
         wait_for(dyb.at[k, :, c], s_dyr.at[k])
@@ -246,7 +260,8 @@
             wait_for(xo, s_misc.at[S_XO])
             wait_for(xp.at[0:ROWS_FIRST], s_misc.at[S_XIN])
             wait_for(xp.at[ROWS_FIRST:ROWS_IN], s_misc.at[S_XIN2])
-            wait_for(xp.at[ROWS_IN:], s_misc.at[S_XOUT])
+            wait_for(xp.at[ROWS_IN:rows_direct], s_misc.at[S_XOUT])
+            wait_for(xp.at[0 : 3 * ROWS_SHARED], s_misc.at[S_XSR])
 
         wait_for(wb.at[k, :, oc], s_sib.at[k])
 
@@ -288,6 +303,7 @@
     @pl.loop(0, LAST + (chunks + 1) // 2)
     def _(t):
         once(t, ROUND, second_round)
+        once(t, SHARE, share_tokens)
         staged(stage_c, t - LAG_C, ring)
         staged(stage_d, t - LAG_D, ring)
         staged(stage_ring, t, ring)
@@ -306,7 +322,9 @@
     wait_for(dyb.at[:, :, 0], s_misc.at[S_DYFS])
     wait_for(xp.at[0:ROWS_FIRST], s_misc.at[S_XS1])
     wait_for(xp.at[ROWS_FIRST:ROWS_IN], s_misc.at[S_XS3])
-    wait_for(xp.at[ROWS_IN:], s_misc.at[S_XS2])
+    wait_for(xp.at[ROWS_IN:rows_direct], s_misc.at[S_XS2])
+    wait_for(xp.at[0:ROWS_SHARED], s_misc.at[S_XSS])
+    wait_for(xp.at[0 : 3 * ROWS_SHARED], s_misc.at[S_XSRS])
     wait_for(cts.at[:, 0 : 4 * LANES], s_misc.at[S_CTS])
     wait_for(cts.at[:, three], s_misc.at[S_CTRS])
     wait_for(sall.at[:, 0 : 4 * LANES], s_misc.at[S_SS])

time: 84.8 us -> 83.6 us (0.986)
  Pallas kernels: 75.3 us -> 74.2 us
    pallas_call x1, Pallas kernels: 75.3 us -> 74.2 us  [local(): pl.pallas_call(functools.partial(kernel, clip_bound, tokens_all), out_sha...]
where the time goes in v5:
time: 83.6 us; the launch traced here: 83.4 us
  Pallas kernels  74.2 us (89%)
  local copies, waits for them, and re-layouts  7.89 us (9%)
  between operations  1.3 us (2%)
    pallas_call x1, Pallas kernels, local(): pl.pallas_call(functools.partial(kernel, clip_bound, tokens_all), out_sha...  74.2 us
    unnamed x11, local copies, waits for them, and re-layouts  7.89 us

profile of v5, /device:TPU:0, one launch (start us, length us, event | category | flops | bytes accessed | tf_op | source)
XLA Modules:
  0.0 83.4 jit_solution(3034162669986169983)
XLA Ops:
  1.3 0.0 copy-start
  1.3 1.5 %copy-done = f32[256,1920]{1,0:T(8,128)S(1)} copy-done((f32[256,1920]{1,0:T(8,128)S(1)}, f32[256,1920]{1,0:T(8,128)}, u32[]{:S(2)}) %copy-start) | copy-done | bytes 1966104
  2.8 0.0 copy-start.1
  2.8 1.2 %copy-done.1 = bf16[256,1920]{1,0:T(8,128)(2,1)S(1)} copy-done((bf16[256,1920]{1,0:T(8,128)(2,1)S(1)}, bf16[256,1920]{1,0:T(8,128)(2,1)}, u32[]{:S(2)}) %copy-start.1) | copy-done | bytes 983064
  4.0 0.0 copy-start.2
  4.0 0.8 %copy-done.2 = bf16[128,256]{1,0:T(8,128)(2,1)S(1)} copy-done((bf16[128,256]{1,0:T(8,128)(2,1)S(1)}, bf16[128,256]{1,0:T(8,128)(2,1)}, u32[]{:S(2)}) %copy-start.2) | copy-done | bytes 65560
  4.9 0.0 copy-start.3
  4.9 0.7 copy-done.3
  5.5 74.2 %step.1 = (f32[256,1920]{1,0:T(8,128)S(1)}, f32[256,1920]{1,0:T(8,128)S(1)}, bf16[384,1920]{1,0:T(8,128)(2,1)S(1)}) custom-call(s32[1]{0:T(128)S(6)} %copy.14.newest, f32[8]{0:T(128)S(1)} %copy-done.3, f32[256,1920]{1,0:T(8,128)S(1)} %copy-done, f32[7,256,1920]{2,1,0:T(8,128)} %history.1, bf16[256,1920]{1,0:T(8,128)(2,1)S(1)} %copy-done.1, ...), custom_call_target="tpu_custom_call" | custom-call | tf_op jit(solution)/shard_map/step/pallas_call | solution.py:353
  79.7 1.3 %copy.15 = f32[256,1920]{1,0:T(8,128)} copy(f32[256,1920]{1,0:T(8,128)S(1)} %get-tuple-element.6) | data formatting | bytes 3932160
  81.0 1.3 %copy.16 = f32[256,1920]{1,0:T(8,128)} copy(f32[256,1920]{1,0:T(8,128)S(1)} %get-tuple-element.7) | data formatting | bytes 3932160
  82.3 1.1 %copy.17 = bf16[384,1920]{1,0:T(8,128)(2,1)} copy(bf16[384,1920]{1,0:T(8,128)(2,1)S(1)} %get-tuple-element.8) | data formatting | bytes 2949120
Async XLA Ops:
  1.3 1.5 %copy-start = (f32[256,1920]{1,0:T(8,128)S(1)}, f32[256,1920]{1,0:T(8,128)}, u32[]{:S(2)}) copy-start(f32[256,1920]{1,0:T(8,128)} %weight.1) | copy-start | bytes 5898244
  2.8 1.2 %copy-start.1 = (bf16[256,1920]{1,0:T(8,128)(2,1)S(1)}, bf16[256,1920]{1,0:T(8,128)(2,1)}, u32[]{:S(2)}) copy-start(bf16[256,1920]{1,0:T(8,128)(2,1)} %fresh.1) | copy-start | bytes 2949124
  4.0 0.8 %copy-start.2 = (bf16[128,256]{1,0:T(8,128)(2,1)S(1)}, bf16[128,256]{1,0:T(8,128)(2,1)}, u32[]{:S(2)}) copy-start(bf16[128,256]{1,0:T(8,128)(2,1)} %x_grad.1) | copy-start | bytes 196612
  4.9 0.7 copy-start.3

commit v6 on v5

--- a/solution.py
+++ b/solution.py
@@ -13,7 +13,7 @@
 noise_multiplier = 0.01
 
 LANES = 128
-ROWS_IN = 144
+ROWS_IN = 192
 ROWS_SHARED = 32
 ROWS_FIRST = 32
 SPECIAL = 4

time: 83.6 us -> 79.4 us (0.950)
  Pallas kernels: 74.2 us -> 70 us
    pallas_call x1, Pallas kernels: 74.2 us -> 70 us  [local(): pl.pallas_call(functools.partial(kernel, clip_bound, tokens_all), out_sha...]
where the time goes in v6:
time: 79.4 us; the launch traced here: 79.2 us
  Pallas kernels  70 us (88%)
  local copies, waits for them, and re-layouts  7.89 us (10%)
  between operations  1.3 us (2%)
    pallas_call x1, Pallas kernels, local(): pl.pallas_call(functools.partial(kernel, clip_bound, tokens_all), out_sha...  70 us
    unnamed x11, local copies, waits for them, and re-layouts  7.89 us

profile of v6, /device:TPU:0, one launch (start us, length us, event | category | flops | bytes accessed | tf_op | source)
XLA Modules:
  0.0 79.2 jit_solution(11543503698406087184)
XLA Ops:
  1.3 0.0 copy-start
  1.3 1.5 %copy-done = f32[256,1920]{1,0:T(8,128)S(1)} copy-done((f32[256,1920]{1,0:T(8,128)S(1)}, f32[256,1920]{1,0:T(8,128)}, u32[]{:S(2)}) %copy-start) | copy-done | bytes 1966104
  2.8 0.0 copy-start.1
  2.8 1.2 %copy-done.1 = bf16[256,1920]{1,0:T(8,128)(2,1)S(1)} copy-done((bf16[256,1920]{1,0:T(8,128)(2,1)S(1)}, bf16[256,1920]{1,0:T(8,128)(2,1)}, u32[]{:S(2)}) %copy-start.1) | copy-done | bytes 983064
  4.0 0.0 copy-start.2
  4.0 0.8 %copy-done.2 = bf16[128,256]{1,0:T(8,128)(2,1)S(1)} copy-done((bf16[128,256]{1,0:T(8,128)(2,1)S(1)}, bf16[128,256]{1,0:T(8,128)(2,1)}, u32[]{:S(2)}) %copy-start.2) | copy-done | bytes 65560
  4.9 0.0 copy-start.3
  4.9 0.7 copy-done.3
  5.5 70.0 %step.1 = (f32[256,1920]{1,0:T(8,128)S(1)}, f32[256,1920]{1,0:T(8,128)S(1)}, bf16[384,1920]{1,0:T(8,128)(2,1)S(1)}) custom-call(s32[1]{0:T(128)S(6)} %copy.14.newest, f32[8]{0:T(128)S(1)} %copy-done.3, f32[256,1920]{1,0:T(8,128)S(1)} %copy-done, f32[7,256,1920]{2,1,0:T(8,128)} %history.1, bf16[256,1920]{1,0:T(8,128)(2,1)S(1)} %copy-done.1, ...), custom_call_target="tpu_custom_call" | custom-call | tf_op jit(solution)/shard_map/step/pallas_call | solution.py:353
  75.5 1.3 %copy.15 = f32[256,1920]{1,0:T(8,128)} copy(f32[256,1920]{1,0:T(8,128)S(1)} %get-tuple-element.6) | data formatting | bytes 3932160
  76.8 1.3 %copy.16 = f32[256,1920]{1,0:T(8,128)} copy(f32[256,1920]{1,0:T(8,128)S(1)} %get-tuple-element.7) | data formatting | bytes 3932160
  78.1 1.1 %copy.17 = bf16[384,1920]{1,0:T(8,128)(2,1)} copy(bf16[384,1920]{1,0:T(8,128)(2,1)S(1)} %get-tuple-element.8) | data formatting | bytes 2949120
Async XLA Ops:
  1.3 1.5 %copy-start = (f32[256,1920]{1,0:T(8,128)S(1)}, f32[256,1920]{1,0:T(8,128)}, u32[]{:S(2)}) copy-start(f32[256,1920]{1,0:T(8,128)} %weight.1) | copy-start | bytes 5898244
  2.8 1.2 %copy-start.1 = (bf16[256,1920]{1,0:T(8,128)(2,1)S(1)}, bf16[256,1920]{1,0:T(8,128)(2,1)}, u32[]{:S(2)}) copy-start(bf16[256,1920]{1,0:T(8,128)(2,1)} %fresh.1) | copy-start | bytes 2949124
  4.0 0.8 %copy-start.2 = (bf16[128,256]{1,0:T(8,128)(2,1)S(1)}, bf16[128,256]{1,0:T(8,128)(2,1)}, u32[]{:S(2)}) copy-start(bf16[128,256]{1,0:T(8,128)(2,1)} %x_grad.1) | copy-start | bytes 196612
  4.9 0.7 copy-start.3
